TPU v7x, 512 devices: a whole 4x8x8 slice. The times are simulated.
512 devices in a mesh: section: 16 (over z, core), seq: 32 (over y, x).
Axes of the slice: x: 4, y: 8, z: 8, core: 2. Of those that a mesh axis runs over, the one named last changes fastest.
Arguments:
- query: bfloat16 [16384, 4096], P('seq', 'section'), may hold values from -6 to 6
- key_proj: bfloat16 [16384, 4096], P('seq', 'section'), may hold values from -6 to 6
- value_proj: bfloat16 [16384, 4096], P('seq', 'section'), may hold values from -6 to 6
- filter_taps: float32 [16384, 4096], P('seq', 'section'), may hold values from -2 to 2
- skip_gain: float32 [4096], P('section'), may hold values from -4 to 4
Outputs:
- handed_on: bfloat16 [16384, 4096], P('seq', 'section')
All inputs are finite; a program needn't handle non-finite values.
Results may differ from a plain program's by a relative error of at most 0.00155.
Values may be sent and summed in bfloat16 or wider, within the bound.
No kernel may reach another device: no remote copies, remote signals or barrier semaphores. Data moves between devices by JAX's collectives and lax.ppermute only.
A program may use at most 64 MiB of HBM per device.

v0:
```python
import jax
import jax.numpy as jnp
import numpy as np
from jax import lax
from jax.experimental import pallas as pl
from jax.experimental.pallas import tpu as pltpu
from jax.sharding import PartitionSpec as P

F16_TOP = 14.0
SCALE_LANES = 128


def passed_along(value, axis, by):
    length = lax.axis_size(axis)
    return lax.ppermute(value, axis, [(i, (i + by) % length) for i in range(length)])


def regrouped(blocks):
    return lax.all_to_all(blocks, "seq", split_axis=0, concat_axis=0, tiled=True)


def split_bf16(table):
    high = table.astype(jnp.bfloat16)
    return high, (table - high.astype(np.float64)).astype(jnp.bfloat16)


def tables(shards, group, tok_rows):
    total = shards * tok_rows
    lanes = 128
    tiles = tok_rows // lanes
    s = np.arange(shards)
    k = np.arange(shards) + 0.25
    own = np.eye(group)
    phase = 2.0 * np.pi * np.outer(k, s) / shards
    cosine, sine = np.kron(np.cos(phase), own), np.kron(np.sin(phase), own)
    fwd_rows = np.concatenate([cosine, -sine], axis=0)
    inv_rows = np.concatenate([cosine.T, -sine.T], axis=1) / total
    b = np.arange(lanes)
    turn = 2.0 * np.pi * np.outer(b, b) / lanes
    c, n = np.cos(turn), np.sin(turn)
    fwd_lanes = np.block([[c, -n], [n, c]])
    inv_lanes = np.block([[c, n], [-n, c]])
    near = np.repeat(2.0 * np.pi * np.outer(k, np.arange(tiles)) / (shards * tiles), lanes, axis=1)
    freq = k[:, None] + shards * np.repeat(np.arange(tiles), lanes)[None, :]
    far = 2.0 * np.pi * freq * np.tile(b, tiles)[None, :] / total
    twiddles = np.stack([np.cos(near), np.sin(near), np.cos(far), np.sin(far)])[:, :, None, :].astype(np.float32)
    rows_high, rows_low = split_bf16(fwd_rows)
    back_high, back_low = split_bf16(inv_rows)
    lane_high, lane_low = split_bf16(fwd_lanes)
    home_high, home_low = split_bf16(inv_lanes)
    return (
        np.concatenate([rows_high, rows_low], axis=1),
        np.concatenate([back_high, back_low], axis=1),
        np.concatenate([lane_high, lane_low], axis=0),
        np.concatenate([home_high, home_low], axis=0),
        twiddles,
    )


def halves(value):
    high = value.astype(jnp.bfloat16)
    low = (value - high.astype(jnp.float32)).astype(jnp.bfloat16)
    return high, low


def left_product(table_ref, value):
    high, low = halves(value)
    depth = value.shape[0]
    table = jnp.concatenate([table_ref[:, :depth], table_ref[:, :depth], table_ref[:, depth:]], axis=1)
    return jnp.dot(table, jnp.concatenate([high, low, high], axis=0), preferred_element_type=jnp.float32)


def right_product(value, table_ref):
    high, low = halves(value)
    depth = value.shape[1]
    table = jnp.concatenate([table_ref[:depth], table_ref[:depth], table_ref[depth:]], axis=0)
    return jnp.dot(jnp.concatenate([high, low, high], axis=1), table, preferred_element_type=jnp.float32)


def tile_of(value, index):
    return value[:, index * 128 : (index + 1) * 128]


def turned(real, imag, cosine, sine):
    return real * cosine - imag * sine, real * sine + imag * cosine


def four_point(r, q, sign):
    r02, q02, r13, q13 = r[0] + r[2], q[0] + q[2], r[1] + r[3], q[1] + q[3]
    d02, e02, d13, e13 = r[0] - r[2], q[0] - q[2], r[1] - r[3], q[1] - q[3]
    reals = [r02 + r13, d02 - sign * e13, r02 - r13, d02 + sign * e13]
    imags = [q02 + q13, e02 + sign * d13, q02 - q13, e02 - sign * d13]
    return reals, imags


def phase(tw_ref, part, tile, group):
    rows = tw_ref[part, :, :, tile * 128 : (tile + 1) * 128]
    count = rows.shape[0]
    return jnp.broadcast_to(rows, (count, group, 128)).reshape(count * group, 128)


def spectrum(value, rows_ref, lanes_ref, tw_ref):
    half = value.shape[0]
    group = half // tw_ref.shape[1]
    both = left_product(rows_ref, value)
    reals, imags = [tile_of(both[:half], 0)], [tile_of(both[half:], 0)]
    for j in range(1, 4):
        real, imag = turned(
            tile_of(both[:half], j),
            tile_of(both[half:], j),
            phase(tw_ref, 0, j, group),
            -phase(tw_ref, 1, j, group),
        )
        reals.append(real)
        imags.append(imag)
    reals, imags = four_point(reals, imags, -1.0)
    out = []
    for m in range(4):
        real, imag = turned(reals[m], imags[m], phase(tw_ref, 2, m, group), -phase(tw_ref, 3, m, group))
        out.append(right_product(jnp.concatenate([real, imag], axis=1), lanes_ref))
    return out


def wire_scale(rows):
    top = jnp.maximum(jnp.max(jnp.abs(rows), axis=1, keepdims=True), 1e-30)
    return F16_TOP - jnp.ceil(jnp.log2(top))


def as_lanes(column):
    return jnp.broadcast_to(column, (column.shape[0], SCALE_LANES))


def pack_kernel(key_hbm, value_hbm, taps_hbm, out_ref, key_ref, value_ref, taps_ref, sems):
    copies = [
        pltpu.make_async_copy(source, target, sems.at[i])
        for i, (source, target) in enumerate(
            [(key_hbm, key_ref), (value_hbm, value_ref), (taps_hbm, taps_ref)]
        )
    ]
    for copy in copies:
        copy.start()
    for copy in copies:
        copy.wait()
    span = key_ref.shape[0]
    driven = key_ref[...].astype(jnp.float32) * value_ref[...].astype(jnp.float32)
    sig, tap = driven.T, taps_ref[...].T
    sig_exp, tap_exp = wire_scale(sig), wire_scale(tap)
    out_ref[:, :span] = sig * jnp.exp2(sig_exp)
    out_ref[:, span : 2 * span] = tap * jnp.exp2(tap_exp)
    lane = lax.broadcasted_iota(jnp.int32, (sig.shape[0], SCALE_LANES), 1)
    out_ref[:, 2 * span :] = jnp.where(lane == 0, as_lanes(sig_exp), as_lanes(tap_exp))


def convolve_kernel(in_ref, rows_ref, back_ref, lanes_ref, home_ref, tw_ref, out_ref):
    span = tw_ref.shape[3]
    sig_in = in_ref[:, :span] * jnp.exp2(-in_ref[:, 2 * span : 2 * span + 1])
    tap_in = in_ref[:, span : 2 * span] * jnp.exp2(-in_ref[:, 2 * span + 1 : 2 * span + 2])
    sig = spectrum(sig_in, rows_ref, lanes_ref, tw_ref)
    tap = spectrum(tap_in, rows_ref, lanes_ref, tw_ref)
    group = in_ref.shape[0] // tw_ref.shape[1]
    reals, imags = [], []
    for m in range(4):
        real, imag = turned(sig[m][:, :128], sig[m][:, 128:], tap[m][:, :128], tap[m][:, 128:])
        back = right_product(jnp.concatenate([real, imag], axis=1), home_ref)
        real, imag = turned(back[:, :128], back[:, 128:], phase(tw_ref, 2, m, group), phase(tw_ref, 3, m, group))
        reals.append(real)
        imags.append(imag)
    reals, imags = four_point(reals, imags, 1.0)
    for j in range(1, 4):
        reals[j], imags[j] = turned(reals[j], imags[j], phase(tw_ref, 0, j, group), phase(tw_ref, 1, j, group))
    real, imag = jnp.concatenate(reals, axis=1), jnp.concatenate(imags, axis=1)
    conv = left_product(back_ref, jnp.concatenate([real, imag], axis=0))
    conv_exp = wire_scale(conv)
    out_ref[:, :span] = conv * jnp.exp2(conv_exp)
    out_ref[:, span:] = as_lanes(conv_exp)


def mix_kernel(conv_ref, query_ref, key_ref, value_ref, gain_ref, out_ref):
    span = query_ref.shape[0]
    conv = (conv_ref[:, :span] * jnp.exp2(-conv_ref[:, span : span + 1])).T
    driven = key_ref[...].astype(jnp.float32) * value_ref[...].astype(jnp.float32)
    mixed = query_ref[...].astype(jnp.float32) * (conv + gain_ref[...] * driven)
    out_ref[...] = mixed.astype(jnp.bfloat16)


def call(kernel, shape, dtype, name, vmem_mib, **more):
    return pl.pallas_call(
        kernel,
        out_shape=jax.ShapeDtypeStruct(shape, dtype),
        compiler_params=pltpu.CompilerParams(vmem_limit_bytes=vmem_mib * 2**20),
        name=name,
        **more,
    )


def on_wire(rows, shards):
    wide = rows.astype(jnp.float16).reshape(shards, rows.shape[0] // shards, rows.shape[1])
    return regrouped(wide).reshape(rows.shape).astype(jnp.float32)


def on_device(query, key_proj, value_proj, filter_taps, skip_gain):
    span, width = query.shape
    shards = lax.axis_size("seq")
    group = width // shards
    packed = call(
        pack_kernel,
        (width, 2 * span + SCALE_LANES),
        jnp.float32,
        "pack",
        12,
        in_specs=[pl.BlockSpec(memory_space=pltpu.HBM)] * 3,
        scratch_shapes=[
            pltpu.VMEM((span, width), jnp.bfloat16),
            pltpu.VMEM((span, width), jnp.bfloat16),
            pltpu.VMEM((span, width), jnp.float32),
            pltpu.SemaphoreType.DMA((3,)),
        ],
    )(*[pltpu.with_memory_space_constraint(a, pltpu.HBM) for a in (key_proj, value_proj, filter_taps)])
    conv = call(convolve_kernel, (width, span + SCALE_LANES), jnp.float32, "convolve", 28)(
        on_wire(packed, shards), *tables(shards, group, span)
    )
    mixed = call(mix_kernel, (span, width), jnp.bfloat16, "mix", 12)(
        on_wire(conv, shards), query, key_proj, value_proj, skip_gain[None, :]
    )
    return passed_along(mixed, "section", 1)


def solution(mesh):
    placed = (
        P("seq", "section"),
        P("seq", "section"),
        P("seq", "section"),
        P("seq", "section"),
        P("section"),
    )
    return jax.shard_map(
        on_device, mesh=mesh, in_specs=placed, out_specs=P("seq", "section"), check_vma=False
    )
```

profile of v0, /device:TPU:2, one launch (start us, length us, event | category | flops | bytes accessed | tf_op | source)
XLA Modules:
  0.0 62.8 jit_solution(16163416963059613043)
XLA Ops:
  0.0 1.7 %pack.1 = f32[256,1152]{1,0:T(8,128)S(1)} custom-call(bf16[512,256]{1,0:T(8,128)(2,1)} %key_ref.1, bf16[512,256]{1,0:T(8,128)(2,1)} %value_ref.1, f32[512,256]{1,0:T(8,128)} %taps_hbm.1), custom_call_target="tpu_custom_call" | custom-call | tf_op jit(solution)/shard_map/pack/pallas_call | solution.py:205
  1.7 0.1 convert_bitcast_fusion
  1.8 0.0 copy-start.2
  1.8 0.0 copy-start.3
  1.8 0.0 copy-start.4
  1.8 0.0 copy-start.5
  1.8 0.0 copy-start.6
  1.9 28.4 %all_to_all.10 = f16[32,8,1152]{2,1,0:T(8,128)(2,1)S(1)} all-to-all(f16[32,8,1152]{2,1,0:T(8,128)(2,1)S(1)} %convert_bitcast_fusion), channel_id=1, replica_groups=mesh['section'=16,'seq'=32] {'seq'}, dimensions={0} | all-to-all | bytes 1179648 | tf_op jit(solution)/shard_map/all_to_all | solution.py:19
  30.3 0.1 bitcast_convert_fusion.in_ref
  30.3 0.0 copy-done.2
  30.4 0.0 copy-done.3
  30.4 0.0 copy-done.4
  30.4 0.0 copy-done.5
  30.4 0.0 copy-done.6
  30.4 3.7 %convolve.1 = f32[256,640]{1,0:T(8,128)S(1)} custom-call(f32[256,1152]{1,0:T(8,128)S(1)} %bitcast_convert_fusion.in_ref, bf16[512,512]{1,0:T(8,128)(2,1)S(1)} %copy-done.3, bf16[256,1024]{1,0:T(8,128)(2,1)S(1)} %copy-done.2, bf16[512,256]{1,0:T(8,128)(2,1)S(1)} %copy-done.6, bf16[512,256]{1,0:T(8,128)(2,1)S(1)} %copy-done.5, f32[4,32,1,512]{3,2,1,0:T(1,128)S(1)} %copy-done.4), custom_call_target="tpu_custom_call" | custom-call | tf_op jit(solution)/shard_map/convolve/pallas_call | solution.py:219
  34.1 0.0 copy-start
  34.1 0.0 copy-start.1
  34.1 0.0 copy-start.7
  34.1 0.0 copy-start.8
  34.2 17.2 %all_to_all.11 = f16[32,8,640]{2,1,0:T(8,128)(2,1)S(1)} all-to-all(f16[32,8,640]{2,1,0:T(8,128)(2,1)S(1)} %convert_bitcast_fusion.1), channel_id=1, replica_groups=mesh['section'=16,'seq'=32] {'seq'}, dimensions={0} | all-to-all | bytes 655360 | tf_op jit(solution)/shard_map/all_to_all | solution.py:19
  51.5 0.3 mix.1
  51.8 0.0 collective-permute-start
  51.8 10.3 %collective-permute-done = bf16[512,256]{1,0:T(8,128)(2,1)S(1)} collective-permute-done((bf16[512,256]{1,0:T(8,128)(2,1)S(1)}, bf16[512,256]{1,0:T(8,128)(2,1)S(1)}, u32[]{:S(2)}, u32[]{:S(2)}) %collective-permute-start) | collective-permute-done | bytes 262176 | tf_op jit(solution)/shard_map/ppermute | solution.py:15
  62.1 0.7 %copy.12 = bf16[512,256]{1,0:T(8,128)(2,1)} copy(bf16[512,256]{1,0:T(8,128)(2,1)S(1)} %collective-permute-done) | data formatting | bytes 524288
  (6 shorter events, 0.1 us)
Async XLA Ops:
  1.8 28.6 %copy-start.2 = (bf16[256,1024]{1,0:T(8,128)(2,1)S(1)}, bf16[256,1024]{1,0:T(8,128)(2,1)}, u32[]{:S(2)}) copy-start(bf16[256,1024]{1,0:T(8,128)(2,1)} %constant.11.clone.back_ref) | copy-start | bytes 1572868
  1.8 28.6 %copy-start.3 = (bf16[512,512]{1,0:T(8,128)(2,1)S(1)}, bf16[512,512]{1,0:T(8,128)(2,1)}, u32[]{:S(2)}) copy-start(bf16[512,512]{1,0:T(8,128)(2,1)} %constant.10.clone.rows_ref) | copy-start | bytes 1572868
  1.8 28.6 %copy-start.4 = (f32[4,32,1,512]{3,2,1,0:T(1,128)S(1)}, f32[4,32,1,512]{3,2,1,0:T(1,128)}, u32[]{:S(2)}) copy-start(f32[4,32,1,512]{3,2,1,0:T(1,128)} %constant.14.clone.tw_ref) | copy-start | bytes 786436
  1.8 28.6 %copy-start.5 = (bf16[512,256]{1,0:T(8,128)(2,1)S(1)}, bf16[512,256]{1,0:T(8,128)(2,1)}, u32[]{:S(2)}) copy-start(bf16[512,256]{1,0:T(8,128)(2,1)} %constant.13.clone.home_ref) | copy-start | bytes 786436
  1.8 28.6 %copy-start.6 = (bf16[512,256]{1,0:T(8,128)(2,1)S(1)}, bf16[512,256]{1,0:T(8,128)(2,1)}, u32[]{:S(2)}) copy-start(bf16[512,256]{1,0:T(8,128)(2,1)} %constant.12.clone.lanes_ref) | copy-start | bytes 786436
  34.1 17.4 %copy-start = (bf16[512,256]{1,0:T(8,128)(2,1)S(1)}, bf16[512,256]{1,0:T(8,128)(2,1)}, u32[]{:S(2)}) copy-start(bf16[512,256]{1,0:T(8,128)(2,1)} %key_ref.1) | copy-start | bytes 786436
  34.1 17.4 %copy-start.1 = (bf16[512,256]{1,0:T(8,128)(2,1)S(1)}, bf16[512,256]{1,0:T(8,128)(2,1)}, u32[]{:S(2)}) copy-start(bf16[512,256]{1,0:T(8,128)(2,1)} %value_ref.1) | copy-start | bytes 786436
  34.1 17.4 %copy-start.7 = (bf16[512,256]{1,0:T(8,128)(2,1)S(1)}, bf16[512,256]{1,0:T(8,128)(2,1)}, u32[]{:S(2)}) copy-start(bf16[512,256]{1,0:T(8,128)(2,1)} %query_ref.1) | copy-start | bytes 786436
  34.1 17.4 %copy-start.8 = (f32[256]{0:T(256)S(1)}, f32[256]{0:T(256)}, u32[]{:S(2)}) copy-start(f32[256]{0:T(256)} %param.14) | copy-start | bytes 3076
  51.8 10.3 %collective-permute-start = (bf16[512,256]{1,0:T(8,128)(2,1)S(1)}, bf16[512,256]{1,0:T(8,128)(2,1)S(1)}, u32[]{:S(2)}, u32[]{:S(2)}) collective-permute-start(bf16[512,256]{1,0:T(8,128)(2,1)S(1)} %mix.1), channel_id=1, source_target_pairs={{0,32},{32,64},{64,96},{96,128},{128,160},{160,192},{192,224},{224... | collective-permute-start | bytes 786440 | tf_op jit(solution)/shard_map/ppermute | solution.py:15
where the time goes:
time: 63 us; the launch traced here: 62.8 us
  blocking collectives  45.6 us (72%)
  waiting for transfers between devices  10.3 us (16%)
  Pallas kernels  5.68 us (9%)
  local copies, waits for them, and re-layouts  0.76 us (1%)
    all_to_all x2, blocking collectives, regrouped(): lax.all_to_all(blocks, 'seq', split_axis=0, concat_axis=0, tiled=True)  45.6 us
    ppermute x1, waiting for transfers between devices, passed_along(): lax.ppermute(value, axis, [(i, (i + by) % length) for i in range(length)])  10.3 us
    pallas_call x1, Pallas kernels, on_device(): call(convolve_kernel, (width, span + SCALE_LANES), jnp.float32, 'convolve...  3.65 us
    pallas_call x1, Pallas kernels, on_device(): call(pack_kernel, (width, 2 * span + SCALE_LANES), jnp.float32, 'pack', 1...  1.71 us
  transfers between devices with their start and end apart: 1, of which 1 were waited for; matrix products, arithmetic and copies ran while one was open for 0% of the time, Pallas kernels for 0%

commit v1 on v0

--- a/solution.py
+++ b/solution.py
@@ -8,6 +8,7 @@
 
 F16_TOP = 14.0
 SCALE_LANES = 128
+FOLD = 4
 
 
 def passed_along(value, axis, by):
@@ -126,38 +127,63 @@
     return F16_TOP - jnp.ceil(jnp.log2(top))
 
 
-def as_lanes(column):
-    return jnp.broadcast_to(column, (column.shape[0], SCALE_LANES))
-
-
-def pack_kernel(key_hbm, value_hbm, taps_hbm, out_ref, key_ref, value_ref, taps_ref, sems):
-    copies = [
-        pltpu.make_async_copy(source, target, sems.at[i])
-        for i, (source, target) in enumerate(
-            [(key_hbm, key_ref), (value_hbm, value_ref), (taps_hbm, taps_ref)]
-        )
-    ]
-    for copy in copies:
+def store_folded(out_ref, fold_ref, parts):
+    rows = out_ref.shape[0]
+    span = parts[0].shape[1]
+    lane = lax.broadcasted_iota(jnp.int32, (rows, SCALE_LANES), 1)
+    tail = jnp.zeros((rows, SCALE_LANES), jnp.float32)
+    for n, part in enumerate(parts):
+        exponent = wire_scale(part)
+        scaled = part * jnp.exp2(exponent)
+        tiles = span // 128
+        for tile in range(tiles):
+            fold_ref[tile] = tile_of(scaled, tile)
+        fold_ref[tiles] = jnp.broadcast_to(exponent, (part.shape[0], SCALE_LANES))
+        for i in range(FOLD):
+            at = (i * len(parts) + n) * span
+            for tile in range(tiles):
+                out_ref[:, at + tile * 128 : at + tile * 128 + 128] = fold_ref[tile, pl.ds(i, rows, stride=FOLD), :]
+            own = fold_ref[tiles, pl.ds(i, rows, stride=FOLD), :]
+            tail = jnp.where(lane == i * len(parts) + n, own, tail)
+    out_ref[:, FOLD * len(parts) * span :] = tail
+
+
+def load_folded(in_ref, fold_ref, count, n):
+    rows, tiles = in_ref.shape[0], fold_ref.shape[0]
+    for i in range(FOLD):
+        lane = FOLD * count * tiles * 128 + i * count + n
+        scale = jnp.exp2(-in_ref[:, lane : lane + 1])
+        for tile in range(tiles):
+            at = ((i * count + n) * tiles + tile) * 128
+            fold_ref[tile, pl.ds(i, rows, stride=FOLD), :] = in_ref[:, at : at + 128] * scale
+    return jnp.concatenate([fold_ref[tile] for tile in range(tiles)], axis=1)
+
+
+def pack_kernel(*refs):
+    count = (len(refs) - 8) // 2
+    sources, outs = refs[: 3 + count], refs[3 + count : 4 + 2 * count]
+    key_ref, value_ref, taps_ref, fold_ref, sems = refs[4 + 2 * count :]
+    targets = (key_ref, value_ref, taps_ref) + outs[1:]
+    copies = [pltpu.make_async_copy(a, b, sems.at[n]) for n, (a, b) in enumerate(zip(sources, targets))]
+    for copy in copies[:3]:
         copy.start()
-    for copy in copies:
+    copies[0].wait()
+    copies[1].wait()
+    driven = key_ref[...].astype(jnp.float32) * value_ref[...].astype(jnp.float32)
+    copies[2].wait()
+    for copy in copies[3:]:
+        copy.start()
+    store_folded(outs[0], fold_ref, [driven.T, taps_ref[...].T])
+    for copy in copies[3:]:
         copy.wait()
-    span = key_ref.shape[0]
-    driven = key_ref[...].astype(jnp.float32) * value_ref[...].astype(jnp.float32)
-    sig, tap = driven.T, taps_ref[...].T
-    sig_exp, tap_exp = wire_scale(sig), wire_scale(tap)
-    out_ref[:, :span] = sig * jnp.exp2(sig_exp)
-    out_ref[:, span : 2 * span] = tap * jnp.exp2(tap_exp)
-    lane = lax.broadcasted_iota(jnp.int32, (sig.shape[0], SCALE_LANES), 1)
-    out_ref[:, 2 * span :] = jnp.where(lane == 0, as_lanes(sig_exp), as_lanes(tap_exp))
-
-
-def convolve_kernel(in_ref, rows_ref, back_ref, lanes_ref, home_ref, tw_ref, out_ref):
-    span = tw_ref.shape[3]
-    sig_in = in_ref[:, :span] * jnp.exp2(-in_ref[:, 2 * span : 2 * span + 1])
-    tap_in = in_ref[:, span : 2 * span] * jnp.exp2(-in_ref[:, 2 * span + 1 : 2 * span + 2])
+
+
+def convolve_kernel(in_ref, rows_ref, back_ref, lanes_ref, home_ref, tw_ref, out_ref, sig_ref, tap_ref, fold_ref):
+    sig_in = load_folded(in_ref, sig_ref, 2, 0)
+    tap_in = load_folded(in_ref, tap_ref, 2, 1)
     sig = spectrum(sig_in, rows_ref, lanes_ref, tw_ref)
     tap = spectrum(tap_in, rows_ref, lanes_ref, tw_ref)
-    group = in_ref.shape[0] // tw_ref.shape[1]
+    group = sig_ref.shape[1] // tw_ref.shape[1]
     reals, imags = [], []
     for m in range(4):
         real, imag = turned(sig[m][:, :128], sig[m][:, 128:], tap[m][:, :128], tap[m][:, 128:])
@@ -170,14 +196,11 @@
         reals[j], imags[j] = turned(reals[j], imags[j], phase(tw_ref, 0, j, group), phase(tw_ref, 1, j, group))
     real, imag = jnp.concatenate(reals, axis=1), jnp.concatenate(imags, axis=1)
     conv = left_product(back_ref, jnp.concatenate([real, imag], axis=0))
-    conv_exp = wire_scale(conv)
-    out_ref[:, :span] = conv * jnp.exp2(conv_exp)
-    out_ref[:, span:] = as_lanes(conv_exp)
-
-
-def mix_kernel(conv_ref, query_ref, key_ref, value_ref, gain_ref, out_ref):
-    span = query_ref.shape[0]
-    conv = (conv_ref[:, :span] * jnp.exp2(-conv_ref[:, span : span + 1])).T
+    store_folded(out_ref, fold_ref, [conv])
+
+
+def mix_kernel(conv_ref, query_ref, key_ref, value_ref, gain_ref, out_ref, fold_ref):
+    conv = load_folded(conv_ref, fold_ref, 1, 0).T
     driven = key_ref[...].astype(jnp.float32) * value_ref[...].astype(jnp.float32)
     mixed = query_ref[...].astype(jnp.float32) * (conv + gain_ref[...] * driven)
     out_ref[...] = mixed.astype(jnp.bfloat16)
@@ -195,31 +218,46 @@
 
 def on_wire(rows, shards):
     wide = rows.astype(jnp.float16).reshape(shards, rows.shape[0] // shards, rows.shape[1])
-    return regrouped(wide).reshape(rows.shape).astype(jnp.float32)
+    return lax.optimization_barrier(regrouped(wide).reshape(rows.shape)).astype(jnp.float32)
 
 
 def on_device(query, key_proj, value_proj, filter_taps, skip_gain):
     span, width = query.shape
     shards = lax.axis_size("seq")
     group = width // shards
-    packed = call(
+    rows = width // FOLD
+    folded = pltpu.VMEM((span // 128 + 1, width, 128), jnp.float32)
+    unfolded = pltpu.VMEM((span // 128, width, 128), jnp.float32)
+    phases = tables(shards, group, span)
+    sources = [
+        pltpu.with_memory_space_constraint(jnp.asarray(a), pltpu.HBM)
+        for a in (key_proj, value_proj, filter_taps) + phases
+    ]
+    wire = jax.ShapeDtypeStruct((rows, 2 * FOLD * span + SCALE_LANES), jnp.float32)
+    packed, *phases = pl.pallas_call(
         pack_kernel,
-        (width, 2 * span + SCALE_LANES),
-        jnp.float32,
-        "pack",
-        12,
-        in_specs=[pl.BlockSpec(memory_space=pltpu.HBM)] * 3,
+        out_shape=[wire] + [jax.ShapeDtypeStruct(a.shape, a.dtype) for a in phases],
+        in_specs=[pl.BlockSpec(memory_space=pltpu.HBM)] * len(sources),
+        out_specs=[pl.BlockSpec(memory_space=pltpu.VMEM)] * (1 + len(phases)),
         scratch_shapes=[
             pltpu.VMEM((span, width), jnp.bfloat16),
             pltpu.VMEM((span, width), jnp.bfloat16),
             pltpu.VMEM((span, width), jnp.float32),
-            pltpu.SemaphoreType.DMA((3,)),
+            folded,
+            pltpu.SemaphoreType.DMA((len(sources),)),
         ],
-    )(*[pltpu.with_memory_space_constraint(a, pltpu.HBM) for a in (key_proj, value_proj, filter_taps)])
-    conv = call(convolve_kernel, (width, span + SCALE_LANES), jnp.float32, "convolve", 28)(
-        on_wire(packed, shards), *tables(shards, group, span)
-    )
-    mixed = call(mix_kernel, (span, width), jnp.bfloat16, "mix", 12)(
+        compiler_params=pltpu.CompilerParams(vmem_limit_bytes=16 * 2**20),
+        name="pack",
+    )(*sources)
+    conv = call(
+        convolve_kernel,
+        (rows, FOLD * span + SCALE_LANES),
+        jnp.float32,
+        "convolve",
+        28,
+        scratch_shapes=[unfolded, unfolded, folded],
+    )(on_wire(packed, shards), *phases)
+    mixed = call(mix_kernel, (span, width), jnp.bfloat16, "mix", 12, scratch_shapes=[unfolded])(
         on_wire(conv, shards), query, key_proj, value_proj, skip_gain[None, :]
     )
     return passed_along(mixed, "section", 1)

time: 63 us -> 62.8 us (level)
  the two profiles are of different devices: /device:TPU:2 before, /device:TPU:16 now
where the time goes in v1:
time: 62.8 us; the launch traced here: 62.6 us
  blocking collectives  43.4 us (69%)
  waiting for transfers between devices  10.6 us (17%)
  Pallas kernels  6.81 us (11%)
  local copies, waits for them, and re-layouts  1.52 us (2%)
    all_to_all x2, blocking collectives, regrouped(): lax.all_to_all(blocks, 'seq', split_axis=0, concat_axis=0, tiled=True)  43.4 us
    ppermute x1, waiting for transfers between devices, passed_along(): lax.ppermute(value, axis, [(i, (i + by) % length) for i in range(length)])  10.6 us
    pallas_call x1, Pallas kernels, on_device(): call(convolve_kernel, (rows, FOLD * span + SCALE_LANES), jnp.float32, 'co...  3.76 us
    pallas_call x1, Pallas kernels, on_device(): pl.pallas_call(pack_kernel, out_shape=[wire] + [jax.ShapeDtypeStruct(a.sh...  2.69 us
  transfers between devices with their start and end apart: 1, of which 1 were waited for; matrix products, arithmetic and copies ran while one was open for 0% of the time, Pallas kernels for 0%

profile of v1, /device:TPU:16, one launch (start us, length us, event | category | flops | bytes accessed | tf_op | source)
XLA Modules:
  0.0 62.6 jit_solution(15504572953998927166)
XLA Ops:
  0.0 2.7 %pack.1 = (f32[64,4224]{1,0:T(8,128)S(1)}, bf16[512,512]{1,0:T(8,128)(2,1)S(1)}, bf16[256,1024]{1,0:T(8,128)(2,1)S(1)}, bf16[512,256]{1,0:T(8,128)(2,1)S(1)}, bf...) custom-call(bf16[512,256]{1,0:T(8,128)(2,1)} %key_ref.1, bf16[512,256]{1,0:T(8,128)(2,1)} %value_ref.1, ...), custom_call_target="tpu_custom_call" | custom-call | tf_op jit(solution)/shard_map/pack/pallas_call | solution.py:237
  2.7 0.1 convert_element_type.12
  2.8 0.3 reshape.12
  3.0 27.0 %all_to_all.10 = f16[32,2,4224]{2,1,0:T(2,128)(2,1)S(1)} all-to-all(f16[32,2,4224]{2,1,0:T(2,128)(2,1)S(1)} %reshape.12), channel_id=1, replica_groups=mesh['section'=16,'seq'=32] {'seq'}, dimensions={0} | all-to-all | bytes 1081344 | tf_op jit(solution)/shard_map/all_to_all | solution.py:20
  30.0 0.3 reshape.13
  30.3 0.1 convert_element_type.13.in_ref
  30.4 3.8 %convolve.1 = f32[64,2176]{1,0:T(8,128)S(1)} custom-call(f32[64,4224]{1,0:T(8,128)S(1)} %convert_element_type.13.in_ref, bf16[512,512]{1,0:T(8,128)(2,1)S(1)} %get-tuple-element.12.rows_ref, bf16[256,1024]{1,0:T(8,128)(2,1)S(1)} %get-tuple-element.13.back_ref, bf16[512,256]{1,0:T(8,128)(2,1)S(1)} %get-tuple-element.14.lanes_ref, ...), custom_call_target="tpu_custom_call" | custom-call | tf_op jit(solution)/shard_map/convolve/pallas_call | solution.py:252
  34.2 0.1 reshape.14
  34.3 0.0 copy-start
  34.3 0.0 copy-start.1
  34.4 0.0 copy-start.2
  34.4 0.0 copy-start.3
  34.4 16.4 %all_to_all.11 = f16[32,2,2176]{2,1,0:T(2,128)(2,1)S(1)} all-to-all(f16[32,2,2176]{2,1,0:T(2,128)(2,1)S(1)} %reshape.14), channel_id=1, replica_groups=mesh['section'=16,'seq'=32] {'seq'}, dimensions={0} | all-to-all | bytes 557056 | tf_op jit(solution)/shard_map/all_to_all | solution.py:20
  50.8 0.1 reshape.15
  50.9 0.0 copy-done
  50.9 0.0 copy-done.1
  51.0 0.0 copy-done.2
  51.0 0.0 copy-done.3
  51.0 0.4 mix.1
  51.3 0.0 collective-permute-start
  51.4 10.6 %collective-permute-done = bf16[512,256]{1,0:T(8,128)(2,1)S(1)} collective-permute-done((bf16[512,256]{1,0:T(8,128)(2,1)S(1)}, bf16[512,256]{1,0:T(8,128)(2,1)S(1)}, u32[]{:S(2)}, u32[]{:S(2)}) %collective-permute-start) | collective-permute-done | bytes 262176 | tf_op jit(solution)/shard_map/ppermute | solution.py:16
  61.9 0.7 %copy.12 = bf16[512,256]{1,0:T(8,128)(2,1)} copy(bf16[512,256]{1,0:T(8,128)(2,1)S(1)} %collective-permute-done) | data formatting | bytes 524288
  (2 shorter events, 0.1 us)
Async XLA Ops:
  34.3 16.6 %copy-start = (bf16[512,256]{1,0:T(8,128)(2,1)S(1)}, bf16[512,256]{1,0:T(8,128)(2,1)}, u32[]{:S(2)}) copy-start(bf16[512,256]{1,0:T(8,128)(2,1)} %key_ref.1) | copy-start | bytes 786436
  34.3 16.6 %copy-start.1 = (bf16[512,256]{1,0:T(8,128)(2,1)S(1)}, bf16[512,256]{1,0:T(8,128)(2,1)}, u32[]{:S(2)}) copy-start(bf16[512,256]{1,0:T(8,128)(2,1)} %value_ref.1) | copy-start | bytes 786436
  34.4 16.6 %copy-start.2 = (bf16[512,256]{1,0:T(8,128)(2,1)S(1)}, bf16[512,256]{1,0:T(8,128)(2,1)}, u32[]{:S(2)}) copy-start(bf16[512,256]{1,0:T(8,128)(2,1)} %query_ref.1) | copy-start | bytes 786436
  34.4 16.6 %copy-start.3 = (f32[256]{0:T(256)S(1)}, f32[256]{0:T(256)}, u32[]{:S(2)}) copy-start(f32[256]{0:T(256)} %param.14) | copy-start | bytes 3076
  51.3 10.6 %collective-permute-start = (bf16[512,256]{1,0:T(8,128)(2,1)S(1)}, bf16[512,256]{1,0:T(8,128)(2,1)S(1)}, u32[]{:S(2)}, u32[]{:S(2)}) collective-permute-start(bf16[512,256]{1,0:T(8,128)(2,1)S(1)} %mix.1), channel_id=1, source_target_pairs={{0,32},{32,64},{64,96},{96,128},{128,160},{160,192},{192,224},{224... | collective-permute-start | bytes 786440 | tf_op jit(solution)/shard_map/ppermute | solution.py:16

commit v2 on v1

--- a/solution.py
+++ b/solution.py
@@ -9,6 +9,7 @@
 F16_TOP = 14.0
 SCALE_LANES = 128
 FOLD = 4
+LAG_NANOS = 3300
 
 
 def passed_along(value, axis, by):
@@ -31,9 +32,9 @@
     tiles = tok_rows // lanes
     s = np.arange(shards)
     k = np.arange(shards) + 0.25
-    own = np.eye(group)
-    phase = 2.0 * np.pi * np.outer(k, s) / shards
-    cosine, sine = np.kron(np.cos(phase), own), np.kron(np.sin(phase), own)
+    own = np.eye(group // FOLD)
+    turn = 2.0 * np.pi * np.outer(k, s) / shards
+    cosine, sine = np.kron(np.cos(turn), own), np.kron(np.sin(turn), own)
     fwd_rows = np.concatenate([cosine, -sine], axis=0)
     inv_rows = np.concatenate([cosine.T, -sine.T], axis=1) / total
     b = np.arange(lanes)
@@ -44,17 +45,17 @@
     near = np.repeat(2.0 * np.pi * np.outer(k, np.arange(tiles)) / (shards * tiles), lanes, axis=1)
     freq = k[:, None] + shards * np.repeat(np.arange(tiles), lanes)[None, :]
     far = 2.0 * np.pi * freq * np.tile(b, tiles)[None, :] / total
-    twiddles = np.stack([np.cos(near), np.sin(near), np.cos(far), np.sin(far)])[:, :, None, :].astype(np.float32)
+    twiddles = np.repeat(np.stack([np.cos(near), np.sin(near), np.cos(far), np.sin(far)]), group // FOLD, axis=1)
     rows_high, rows_low = split_bf16(fwd_rows)
     back_high, back_low = split_bf16(inv_rows)
     lane_high, lane_low = split_bf16(fwd_lanes)
     home_high, home_low = split_bf16(inv_lanes)
     return (
-        np.concatenate([rows_high, rows_low], axis=1),
-        np.concatenate([back_high, back_low], axis=1),
+        np.concatenate([rows_high, rows_high, rows_low], axis=1),
+        np.concatenate([back_high, back_high, back_low], axis=1),
         np.concatenate([lane_high, lane_low], axis=0),
         np.concatenate([home_high, home_low], axis=0),
-        twiddles,
+        twiddles.astype(np.float32),
     )
 
 
@@ -66,9 +67,7 @@
 
 def left_product(table_ref, value):
     high, low = halves(value)
-    depth = value.shape[0]
-    table = jnp.concatenate([table_ref[:, :depth], table_ref[:, :depth], table_ref[:, depth:]], axis=1)
-    return jnp.dot(table, jnp.concatenate([high, low, high], axis=0), preferred_element_type=jnp.float32)
+    return jnp.dot(table_ref[...], jnp.concatenate([high, low, high], axis=0), preferred_element_type=jnp.float32)
 
 
 def right_product(value, table_ref):
@@ -94,30 +93,21 @@
     return reals, imags
 
 
-def phase(tw_ref, part, tile, group):
-    rows = tw_ref[part, :, :, tile * 128 : (tile + 1) * 128]
-    count = rows.shape[0]
-    return jnp.broadcast_to(rows, (count, group, 128)).reshape(count * group, 128)
-
-
-def spectrum(value, rows_ref, lanes_ref, tw_ref):
-    half = value.shape[0]
-    group = half // tw_ref.shape[1]
-    both = left_product(rows_ref, value)
-    reals, imags = [tile_of(both[:half], 0)], [tile_of(both[half:], 0)]
+def phase(tw_ref, part, tile):
+    return jnp.concatenate([tw_ref[part, :, tile * 128 : (tile + 1) * 128]] * FOLD, axis=0)
+
+
+def spectrum(blocks, rows_ref, lanes_ref, tw_ref):
+    half = blocks[0].shape[0]
+    outs = [left_product(rows_ref, block) for block in blocks]
+    reals = [jnp.concatenate([tile_of(out[:half], j) for out in outs], axis=0) for j in range(4)]
+    imags = [jnp.concatenate([tile_of(out[half:], j) for out in outs], axis=0) for j in range(4)]
     for j in range(1, 4):
-        real, imag = turned(
-            tile_of(both[:half], j),
-            tile_of(both[half:], j),
-            phase(tw_ref, 0, j, group),
-            -phase(tw_ref, 1, j, group),
-        )
-        reals.append(real)
-        imags.append(imag)
+        reals[j], imags[j] = turned(reals[j], imags[j], phase(tw_ref, 0, j), -phase(tw_ref, 1, j))
     reals, imags = four_point(reals, imags, -1.0)
     out = []
     for m in range(4):
-        real, imag = turned(reals[m], imags[m], phase(tw_ref, 2, m, group), -phase(tw_ref, 3, m, group))
+        real, imag = turned(reals[m], imags[m], phase(tw_ref, 2, m), -phase(tw_ref, 3, m))
         out.append(right_product(jnp.concatenate([real, imag], axis=1), lanes_ref))
     return out
 
@@ -165,38 +155,54 @@
     key_ref, value_ref, taps_ref, fold_ref, sems = refs[4 + 2 * count :]
     targets = (key_ref, value_ref, taps_ref) + outs[1:]
     copies = [pltpu.make_async_copy(a, b, sems.at[n]) for n, (a, b) in enumerate(zip(sources, targets))]
-    for copy in copies[:3]:
+    for copy in copies:
         copy.start()
     copies[0].wait()
     copies[1].wait()
     driven = key_ref[...].astype(jnp.float32) * value_ref[...].astype(jnp.float32)
     copies[2].wait()
-    for copy in copies[3:]:
-        copy.start()
+
+    @pl.when(lax.axis_index("section") % 2 == 0)
+    def _():
+        pl.delay(LAG_NANOS)
+
     store_folded(outs[0], fold_ref, [driven.T, taps_ref[...].T])
     for copy in copies[3:]:
         copy.wait()
 
 
-def convolve_kernel(in_ref, rows_ref, back_ref, lanes_ref, home_ref, tw_ref, out_ref, sig_ref, tap_ref, fold_ref):
-    sig_in = load_folded(in_ref, sig_ref, 2, 0)
-    tap_in = load_folded(in_ref, tap_ref, 2, 1)
-    sig = spectrum(sig_in, rows_ref, lanes_ref, tw_ref)
-    tap = spectrum(tap_in, rows_ref, lanes_ref, tw_ref)
-    group = sig_ref.shape[1] // tw_ref.shape[1]
+def convolve_kernel(in_ref, rows_ref, back_ref, lanes_ref, home_ref, tw_ref, out_ref):
+    rows, span = in_ref.shape[0], tw_ref.shape[2]
+
+    def part(n):
+        blocks = []
+        for i in range(FOLD):
+            at, lane = (2 * i + n) * span, 2 * FOLD * span + 2 * i + n
+            blocks.append(in_ref[:, at : at + span] * jnp.exp2(-in_ref[:, lane : lane + 1]))
+        return blocks
+
+    sig = spectrum(part(0), rows_ref, lanes_ref, tw_ref)
+    tap = spectrum(part(1), rows_ref, lanes_ref, tw_ref)
     reals, imags = [], []
     for m in range(4):
         real, imag = turned(sig[m][:, :128], sig[m][:, 128:], tap[m][:, :128], tap[m][:, 128:])
         back = right_product(jnp.concatenate([real, imag], axis=1), home_ref)
-        real, imag = turned(back[:, :128], back[:, 128:], phase(tw_ref, 2, m, group), phase(tw_ref, 3, m, group))
+        real, imag = turned(back[:, :128], back[:, 128:], phase(tw_ref, 2, m), phase(tw_ref, 3, m))
         reals.append(real)
         imags.append(imag)
     reals, imags = four_point(reals, imags, 1.0)
     for j in range(1, 4):
-        reals[j], imags[j] = turned(reals[j], imags[j], phase(tw_ref, 0, j, group), phase(tw_ref, 1, j, group))
+        reals[j], imags[j] = turned(reals[j], imags[j], phase(tw_ref, 0, j), phase(tw_ref, 1, j))
     real, imag = jnp.concatenate(reals, axis=1), jnp.concatenate(imags, axis=1)
-    conv = left_product(back_ref, jnp.concatenate([real, imag], axis=0))
-    store_folded(out_ref, fold_ref, [conv])
+    lane = lax.broadcasted_iota(jnp.int32, (rows, SCALE_LANES), 1)
+    tail = jnp.zeros((rows, SCALE_LANES), jnp.float32)
+    for i in range(FOLD):
+        own = slice(i * rows, (i + 1) * rows)
+        conv = left_product(back_ref, jnp.concatenate([real[own], imag[own]], axis=0))
+        exponent = wire_scale(conv)
+        out_ref[:, i * span : (i + 1) * span] = conv * jnp.exp2(exponent)
+        tail = jnp.where(lane == i, exponent, tail)
+    out_ref[:, FOLD * span :] = tail
 
 
 def mix_kernel(conv_ref, query_ref, key_ref, value_ref, gain_ref, out_ref, fold_ref):
@@ -255,7 +261,6 @@
         jnp.float32,
         "convolve",
         28,
-        scratch_shapes=[unfolded, unfolded, folded],
     )(on_wire(packed, shards), *phases)
     mixed = call(mix_kernel, (span, width), jnp.bfloat16, "mix", 12, scratch_shapes=[unfolded])(
         on_wire(conv, shards), query, key_proj, value_proj, skip_gain[None, :]

time: 62.8 us -> 58.2 us (0.927)
  the two profiles are of different devices: /device:TPU:16 before, /device:TPU:193 now
where the time goes in v2:
time: 58.2 us; the launch traced here: 58.1 us
  blocking collectives  39 us (67%)
  starting transfers between devices  8.83 us (15%)
  Pallas kernels  5.08 us (9%)
  waiting for transfers between devices  3.32 us (6%)
  local copies, waits for them, and re-layouts  1.52 us (3%)
    all_to_all x2, blocking collectives, regrouped(): lax.all_to_all(blocks, 'seq', split_axis=0, concat_axis=0, tiled=True)  39 us
    ppermute x1, starting transfers between devices, passed_along(): lax.ppermute(value, axis, [(i, (i + by) % length) for i in range(length)])  8.83 us
    ppermute x1, waiting for transfers between devices, passed_along(): lax.ppermute(value, axis, [(i, (i + by) % length) for i in range(length)])  3.32 us
    pallas_call x1, Pallas kernels, on_device(): call(convolve_kernel, (rows, FOLD * span + SCALE_LANES), jnp.float32, 'co...  2.88 us
    pallas_call x1, Pallas kernels, on_device(): pl.pallas_call(pack_kernel, out_shape=[wire] + [jax.ShapeDtypeStruct(a.sh...  1.84 us
  transfers between devices with their start and end apart: 1, of which 1 were waited for; matrix products, arithmetic and copies ran while one was open for 0% of the time, Pallas kernels for 0%

profile of v2, /device:TPU:193, one launch (start us, length us, event | category | flops | bytes accessed | tf_op | source)
XLA Modules:
  0.0 58.1 jit_solution(10809990426178809646)
XLA Ops:
  0.0 1.8 %pack.1 = (f32[64,4224]{1,0:T(8,128)S(1)}, bf16[128,192]{1,0:T(8,128)(2,1)S(1)}, bf16[64,384]{1,0:T(8,128)(2,1)S(1)}, bf16[512,256]{1,0:T(8,128)(2,1)S(1)}, bf16...) custom-call(bf16[512,256]{1,0:T(8,128)(2,1)} %key_ref.1, bf16[512,256]{1,0:T(8,128)(2,1)} %value_ref.1, ...), custom_call_target="tpu_custom_call" | custom-call | tf_op jit(solution)/shard_map/pack/pallas_call | solution.py:243
  1.8 0.1 convert_element_type.12
  1.9 0.3 reshape.12
  2.2 22.4 %all_to_all.10 = f16[32,2,4224]{2,1,0:T(2,128)(2,1)S(1)} all-to-all(f16[32,2,4224]{2,1,0:T(2,128)(2,1)S(1)} %reshape.12), channel_id=1, replica_groups=mesh['section'=16,'seq'=32] {'seq'}, dimensions={0} | all-to-all | bytes 1081344 | tf_op jit(solution)/shard_map/all_to_all | solution.py:21
  24.6 0.3 reshape.13
  24.8 0.1 convert_element_type.13.in_ref
  24.9 2.9 %convolve.1 = f32[64,2176]{1,0:T(8,128)S(1)} custom-call(f32[64,4224]{1,0:T(8,128)S(1)} %convert_element_type.13.in_ref, bf16[128,192]{1,0:T(8,128)(2,1)S(1)} %get-tuple-element.12.rows_ref, bf16[64,384]{1,0:T(8,128)(2,1)S(1)} %get-tuple-element.13.back_ref, bf16[512,256]{1,0:T(8,128)(2,1)S(1)} %get-tuple-element.14.lanes_ref, ...), custom_call_target="tpu_custom_call" | custom-call | tf_op jit(solution)/shard_map/convolve/pallas_call | solution.py:258
  27.8 0.1 reshape.14
  28.0 0.0 copy-start
  28.0 0.0 copy-start.1
  28.0 0.0 copy-start.2
  28.0 0.0 copy-start.3
  28.0 16.6 %all_to_all.11 = f16[32,2,2176]{2,1,0:T(2,128)(2,1)S(1)} all-to-all(f16[32,2,2176]{2,1,0:T(2,128)(2,1)S(1)} %reshape.14), channel_id=1, replica_groups=mesh['section'=16,'seq'=32] {'seq'}, dimensions={0} | all-to-all | bytes 557056 | tf_op jit(solution)/shard_map/all_to_all | solution.py:21
  44.6 0.1 reshape.15
  44.8 0.0 copy-done
  44.8 0.0 copy-done.1
  44.8 0.0 copy-done.2
  44.8 0.0 copy-done.3
  44.8 0.4 mix.1
  45.2 8.8 %collective-permute-start = (bf16[512,256]{1,0:T(8,128)(2,1)S(1)}, bf16[512,256]{1,0:T(8,128)(2,1)S(1)}, u32[]{:S(2)}, u32[]{:S(2)}) collective-permute-start(bf16[512,256]{1,0:T(8,128)(2,1)S(1)} %mix.1), channel_id=1, source_target_pairs={{0,32},{32,64},{64,96},{96,128},{128,160},{160,192},{192,224},{224... | collective-permute-start | bytes 786440 | tf_op jit(solution)/shard_map/ppermute | solution.py:17
  54.0 3.3 %collective-permute-done = bf16[512,256]{1,0:T(8,128)(2,1)S(1)} collective-permute-done((bf16[512,256]{1,0:T(8,128)(2,1)S(1)}, bf16[512,256]{1,0:T(8,128)(2,1)S(1)}, u32[]{:S(2)}, u32[]{:S(2)}) %collective-permute-start) | collective-permute-done | bytes 262176 | tf_op jit(solution)/shard_map/ppermute | solution.py:17
  57.4 0.7 %copy.12 = bf16[512,256]{1,0:T(8,128)(2,1)} copy(bf16[512,256]{1,0:T(8,128)(2,1)S(1)} %collective-permute-done) | data formatting | bytes 524288
  (2 shorter events, 0.1 us)
Async XLA Ops:
  28.0 16.8 %copy-start = (bf16[512,256]{1,0:T(8,128)(2,1)S(1)}, bf16[512,256]{1,0:T(8,128)(2,1)}, u32[]{:S(2)}) copy-start(bf16[512,256]{1,0:T(8,128)(2,1)} %key_ref.1) | copy-start | bytes 786436
  28.0 16.8 %copy-start.1 = (bf16[512,256]{1,0:T(8,128)(2,1)S(1)}, bf16[512,256]{1,0:T(8,128)(2,1)}, u32[]{:S(2)}) copy-start(bf16[512,256]{1,0:T(8,128)(2,1)} %value_ref.1) | copy-start | bytes 786436
  28.0 16.8 %copy-start.2 = (bf16[512,256]{1,0:T(8,128)(2,1)S(1)}, bf16[512,256]{1,0:T(8,128)(2,1)}, u32[]{:S(2)}) copy-start(bf16[512,256]{1,0:T(8,128)(2,1)} %query_ref.1) | copy-start | bytes 786436
  28.0 16.8 %copy-start.3 = (f32[256]{0:T(256)S(1)}, f32[256]{0:T(256)}, u32[]{:S(2)}) copy-start(f32[256]{0:T(256)} %param.14) | copy-start | bytes 3076
  45.2 12.1 %collective-permute-start = (bf16[512,256]{1,0:T(8,128)(2,1)S(1)}, bf16[512,256]{1,0:T(8,128)(2,1)S(1)}, u32[]{:S(2)}, u32[]{:S(2)}) collective-permute-start(bf16[512,256]{1,0:T(8,128)(2,1)S(1)} %mix.1), channel_id=1, source_target_pairs={{0,32},{32,64},{64,96},{96,128},{128,160},{160,192},{192,224},{224... | collective-permute-start | bytes 786440 | tf_op jit(solution)/shard_map/ppermute | solution.py:17

commit v3 on v2

--- a/solution.py
+++ b/solution.py
@@ -33,10 +33,13 @@
     s = np.arange(shards)
     k = np.arange(shards) + 0.25
     own = np.eye(group // FOLD)
+    fwd_rows = []
+    for j in range(tiles):
+        turn = 2.0 * np.pi * np.outer(k, tiles * s + j) / (shards * tiles)
+        fwd_rows.append(np.concatenate([np.kron(np.cos(turn), own), np.kron(-np.sin(turn), own)], axis=0))
+    fwd_rows = np.stack(fwd_rows)
     turn = 2.0 * np.pi * np.outer(k, s) / shards
-    cosine, sine = np.kron(np.cos(turn), own), np.kron(np.sin(turn), own)
-    fwd_rows = np.concatenate([cosine, -sine], axis=0)
-    inv_rows = np.concatenate([cosine.T, -sine.T], axis=1) / total
+    inv_rows = np.concatenate([np.kron(np.cos(turn), own).T, np.kron(-np.sin(turn), own).T], axis=1) / total
     b = np.arange(lanes)
     turn = 2.0 * np.pi * np.outer(b, b) / lanes
     c, n = np.cos(turn), np.sin(turn)
@@ -51,7 +54,7 @@
     lane_high, lane_low = split_bf16(fwd_lanes)
     home_high, home_low = split_bf16(inv_lanes)
     return (
-        np.concatenate([rows_high, rows_high, rows_low], axis=1),
+        np.concatenate([rows_high, rows_high, rows_low], axis=2),
         np.concatenate([back_high, back_high, back_low], axis=1),
         np.concatenate([lane_high, lane_low], axis=0),
         np.concatenate([home_high, home_low], axis=0),
@@ -65,9 +68,9 @@
     return high, low
 
 
-def left_product(table_ref, value):
+def left_product(table, value):
     high, low = halves(value)
-    return jnp.dot(table_ref[...], jnp.concatenate([high, low, high], axis=0), preferred_element_type=jnp.float32)
+    return jnp.dot(table, jnp.concatenate([high, low, high], axis=0), preferred_element_type=jnp.float32)
 
 
 def right_product(value, table_ref):
@@ -94,22 +97,7 @@
 
 
 def phase(tw_ref, part, tile):
-    return jnp.concatenate([tw_ref[part, :, tile * 128 : (tile + 1) * 128]] * FOLD, axis=0)
-
-
-def spectrum(blocks, rows_ref, lanes_ref, tw_ref):
-    half = blocks[0].shape[0]
-    outs = [left_product(rows_ref, block) for block in blocks]
-    reals = [jnp.concatenate([tile_of(out[:half], j) for out in outs], axis=0) for j in range(4)]
-    imags = [jnp.concatenate([tile_of(out[half:], j) for out in outs], axis=0) for j in range(4)]
-    for j in range(1, 4):
-        reals[j], imags[j] = turned(reals[j], imags[j], phase(tw_ref, 0, j), -phase(tw_ref, 1, j))
-    reals, imags = four_point(reals, imags, -1.0)
-    out = []
-    for m in range(4):
-        real, imag = turned(reals[m], imags[m], phase(tw_ref, 2, m), -phase(tw_ref, 3, m))
-        out.append(right_product(jnp.concatenate([real, imag], axis=1), lanes_ref))
-    return out
+    return tw_ref[part, :, tile * 128 : (tile + 1) * 128]
 
 
 def wire_scale(rows):
@@ -174,34 +162,57 @@
 def convolve_kernel(in_ref, rows_ref, back_ref, lanes_ref, home_ref, tw_ref, out_ref):
     rows, span = in_ref.shape[0], tw_ref.shape[2]
 
-    def part(n):
-        blocks = []
-        for i in range(FOLD):
-            at, lane = (2 * i + n) * span, 2 * FOLD * span + 2 * i + n
-            blocks.append(in_ref[:, at : at + span] * jnp.exp2(-in_ref[:, lane : lane + 1]))
-        return blocks
-
-    sig = spectrum(part(0), rows_ref, lanes_ref, tw_ref)
-    tap = spectrum(part(1), rows_ref, lanes_ref, tw_ref)
-    reals, imags = [], []
-    for m in range(4):
-        real, imag = turned(sig[m][:, :128], sig[m][:, 128:], tap[m][:, :128], tap[m][:, 128:])
-        back = right_product(jnp.concatenate([real, imag], axis=1), home_ref)
-        real, imag = turned(back[:, :128], back[:, 128:], phase(tw_ref, 2, m), phase(tw_ref, 3, m))
-        reals.append(real)
-        imags.append(imag)
-    reals, imags = four_point(reals, imags, 1.0)
-    for j in range(1, 4):
-        reals[j], imags[j] = turned(reals[j], imags[j], phase(tw_ref, 0, j), phase(tw_ref, 1, j))
-    real, imag = jnp.concatenate(reals, axis=1), jnp.concatenate(imags, axis=1)
+    def part(i, n):
+        at, lane = (2 * i + n) * span, 2 * FOLD * span + 2 * i + n
+        return in_ref[:, at : at + span] * jnp.exp2(-in_ref[:, lane : lane + 1])
+
     lane = lax.broadcasted_iota(jnp.int32, (rows, SCALE_LANES), 1)
     tail = jnp.zeros((rows, SCALE_LANES), jnp.float32)
+    exponents, held = [None] * FOLD, [None] * FOLD
+
+    def rows_step(i):
+        sig, tap = part(i, 0), part(i, 1)
+        outs = []
+        for j in range(4):
+            both = jnp.concatenate([tile_of(sig, j), tile_of(tap, j)], axis=1)
+            outs.append(left_product(rows_ref[j], both))
+        held[i] = outs
+
+    def lanes_step(i):
+        reals, imags = four_point([out[:rows] for out in held[i]], [out[rows:] for out in held[i]], -1.0)
+        blocks = []
+        for n in range(2):
+            for m in range(4):
+                cosine, sine = phase(tw_ref, 2, m), phase(tw_ref, 3, m)
+                real, imag = turned(tile_of(reals[m], n), tile_of(imags[m], n), cosine, -sine)
+                blocks.append(jnp.concatenate([real, imag], axis=1))
+        held[i] = right_product(jnp.concatenate(blocks, axis=0), lanes_ref)
+
+    def product_step(i):
+        sig, tap = held[i][: 4 * rows], held[i][4 * rows :]
+        product = turned(sig[:, :128], sig[:, 128:], tap[:, :128], tap[:, 128:])
+        held[i] = right_product(jnp.concatenate(product, axis=1), home_ref)
+
+    def back_step(i):
+        reals, imags = [], []
+        for m in range(4):
+            own = held[i][m * rows : (m + 1) * rows]
+            real, imag = turned(own[:, :128], own[:, 128:], phase(tw_ref, 2, m), phase(tw_ref, 3, m))
+            reals.append(real)
+            imags.append(imag)
+        reals, imags = four_point(reals, imags, 1.0)
+        for j in range(1, 4):
+            reals[j], imags[j] = turned(reals[j], imags[j], phase(tw_ref, 0, j), phase(tw_ref, 1, j))
+        parts = [jnp.concatenate(reals, axis=1), jnp.concatenate(imags, axis=1)]
+        conv = left_product(back_ref[...], jnp.concatenate(parts, axis=0))
+        exponents[i] = wire_scale(conv)
+        out_ref[:, i * span : (i + 1) * span] = conv * jnp.exp2(exponents[i])
+
+    steps = (rows_step, lanes_step, product_step, back_step)
+    for step, i in ((0, 0), (0, 1), (1, 0), (0, 2), (1, 1), (2, 0), (0, 3), (1, 2), (2, 1), (3, 0), (1, 3), (2, 2), (3, 1), (2, 3), (3, 2), (3, 3)):
+        steps[step](i)
     for i in range(FOLD):
-        own = slice(i * rows, (i + 1) * rows)
-        conv = left_product(back_ref, jnp.concatenate([real[own], imag[own]], axis=0))
-        exponent = wire_scale(conv)
-        out_ref[:, i * span : (i + 1) * span] = conv * jnp.exp2(exponent)
-        tail = jnp.where(lane == i, exponent, tail)
+        tail = jnp.where(lane == i, exponents[i], tail)
     out_ref[:, FOLD * span :] = tail
 
 

time: 58.2 us -> 58 us (level)
  no operation moved by 1% of the time
where the time goes in v3:
time: 58 us; the launch traced here: 57.8 us
  blocking collectives  39 us (67%)
  starting transfers between devices  8.82 us (15%)
  Pallas kernels  4.86 us (8%)
  waiting for transfers between devices  3.32 us (6%)
  local copies, waits for them, and re-layouts  1.52 us (3%)
    all_to_all x2, blocking collectives, regrouped(): lax.all_to_all(blocks, 'seq', split_axis=0, concat_axis=0, tiled=True)  39 us
    ppermute x1, starting transfers between devices, passed_along(): lax.ppermute(value, axis, [(i, (i + by) % length) for i in range(length)])  8.82 us
    ppermute x1, waiting for transfers between devices, passed_along(): lax.ppermute(value, axis, [(i, (i + by) % length) for i in range(length)])  3.32 us
    pallas_call x1, Pallas kernels, on_device(): call(convolve_kernel, (rows, FOLD * span + SCALE_LANES), jnp.float32, 'co...  2.66 us
    pallas_call x1, Pallas kernels, on_device(): pl.pallas_call(pack_kernel, out_shape=[wire] + [jax.ShapeDtypeStruct(a.sh...  1.84 us
  transfers between devices with their start and end apart: 1, of which 1 were waited for; matrix products, arithmetic and copies ran while one was open for 0% of the time, Pallas kernels for 0%

profile of v3, /device:TPU:193, one launch (start us, length us, event | category | flops | bytes accessed | tf_op | source)
XLA Modules:
  0.0 57.8 jit_solution(8975285227281357296)
XLA Ops:
  0.0 1.8 %pack.1 = (f32[64,4224]{1,0:T(8,128)S(1)}, bf16[4,128,192]{2,1,0:T(8,128)(2,1)S(1)}, bf16[64,384]{1,0:T(8,128)(2,1)S(1)}, bf16[512,256]{1,0:T(8,128)(2,1)S(1)}, ...) custom-call(bf16[512,256]{1,0:T(8,128)(2,1)} %key_ref.1, bf16[512,256]{1,0:T(8,128)(2,1)} %value_ref.1, ...), custom_call_target="tpu_custom_call" | custom-call | tf_op jit(solution)/shard_map/pack/pallas_call | solution.py:254
  1.8 0.1 convert_element_type.12
  1.9 0.3 reshape.12
  2.2 22.4 %all_to_all.10 = f16[32,2,4224]{2,1,0:T(2,128)(2,1)S(1)} all-to-all(f16[32,2,4224]{2,1,0:T(2,128)(2,1)S(1)} %reshape.12), channel_id=1, replica_groups=mesh['section'=16,'seq'=32] {'seq'}, dimensions={0} | all-to-all | bytes 1081344 | tf_op jit(solution)/shard_map/all_to_all | solution.py:21
  24.6 0.3 reshape.13
  24.8 0.1 convert_element_type.13.in_ref
  24.9 2.7 %convolve.1 = f32[64,2176]{1,0:T(8,128)S(1)} custom-call(f32[64,4224]{1,0:T(8,128)S(1)} %convert_element_type.13.in_ref, bf16[4,128,192]{2,1,0:T(8,128)(2,1)S(1)} %get-tuple-element.12.rows_ref, bf16[64,384]{1,0:T(8,128)(2,1)S(1)} %get-tuple-element.13.back_ref, bf16[512,256]{1,0:T(8,128)(2,1)S(1)} %get-tuple-element.14.lanes_ref, ...), custom_call_target="tpu_custom_call" | custom-call | tf_op jit(solution)/shard_map/convolve/pallas_call | solution.py:269
  27.6 0.1 reshape.14
  27.7 0.0 copy-start
  27.8 0.0 copy-start.1
  27.8 0.0 copy-start.2
  27.8 0.0 copy-start.3
  27.8 16.6 %all_to_all.11 = f16[32,2,2176]{2,1,0:T(2,128)(2,1)S(1)} all-to-all(f16[32,2,2176]{2,1,0:T(2,128)(2,1)S(1)} %reshape.14), channel_id=1, replica_groups=mesh['section'=16,'seq'=32] {'seq'}, dimensions={0} | all-to-all | bytes 557056 | tf_op jit(solution)/shard_map/all_to_all | solution.py:21
  44.4 0.1 reshape.15
  44.6 0.0 copy-done
  44.6 0.0 copy-done.1
  44.6 0.0 copy-done.2
  44.6 0.0 copy-done.3
  44.6 0.4 mix.1
  45.0 8.8 %collective-permute-start = (bf16[512,256]{1,0:T(8,128)(2,1)S(1)}, bf16[512,256]{1,0:T(8,128)(2,1)S(1)}, u32[]{:S(2)}, u32[]{:S(2)}) collective-permute-start(bf16[512,256]{1,0:T(8,128)(2,1)S(1)} %mix.1), channel_id=1, source_target_pairs={{0,32},{32,64},{64,96},{96,128},{128,160},{160,192},{192,224},{224... | collective-permute-start | bytes 786440 | tf_op jit(solution)/shard_map/ppermute | solution.py:17
  53.8 3.3 %collective-permute-done = bf16[512,256]{1,0:T(8,128)(2,1)S(1)} collective-permute-done((bf16[512,256]{1,0:T(8,128)(2,1)S(1)}, bf16[512,256]{1,0:T(8,128)(2,1)S(1)}, u32[]{:S(2)}, u32[]{:S(2)}) %collective-permute-start) | collective-permute-done | bytes 262176 | tf_op jit(solution)/shard_map/ppermute | solution.py:17
  57.1 0.7 %copy.12 = bf16[512,256]{1,0:T(8,128)(2,1)} copy(bf16[512,256]{1,0:T(8,128)(2,1)S(1)} %collective-permute-done) | data formatting | bytes 524288
  (2 shorter events, 0.1 us)
Async XLA Ops:
  27.7 16.8 %copy-start = (bf16[512,256]{1,0:T(8,128)(2,1)S(1)}, bf16[512,256]{1,0:T(8,128)(2,1)}, u32[]{:S(2)}) copy-start(bf16[512,256]{1,0:T(8,128)(2,1)} %key_ref.1) | copy-start | bytes 786436
  27.8 16.8 %copy-start.1 = (bf16[512,256]{1,0:T(8,128)(2,1)S(1)}, bf16[512,256]{1,0:T(8,128)(2,1)}, u32[]{:S(2)}) copy-start(bf16[512,256]{1,0:T(8,128)(2,1)} %value_ref.1) | copy-start | bytes 786436
  27.8 16.8 %copy-start.2 = (bf16[512,256]{1,0:T(8,128)(2,1)S(1)}, bf16[512,256]{1,0:T(8,128)(2,1)}, u32[]{:S(2)}) copy-start(bf16[512,256]{1,0:T(8,128)(2,1)} %query_ref.1) | copy-start | bytes 786436
  27.8 16.8 %copy-start.3 = (f32[256]{0:T(256)S(1)}, f32[256]{0:T(256)}, u32[]{:S(2)}) copy-start(f32[256]{0:T(256)} %param.14) | copy-start | bytes 3076
  45.0 12.1 %collective-permute-start = (bf16[512,256]{1,0:T(8,128)(2,1)S(1)}, bf16[512,256]{1,0:T(8,128)(2,1)S(1)}, u32[]{:S(2)}, u32[]{:S(2)}) collective-permute-start(bf16[512,256]{1,0:T(8,128)(2,1)S(1)} %mix.1), channel_id=1, source_target_pairs={{0,32},{32,64},{64,96},{96,128},{128,160},{160,192},{192,224},{224... | collective-permute-start | bytes 786440 | tf_op jit(solution)/shard_map/ppermute | solution.py:17

commit v4 on v3

--- a/solution.py
+++ b/solution.py
@@ -107,10 +107,11 @@
 
 def store_folded(out_ref, fold_ref, parts):
     rows = out_ref.shape[0]
-    span = parts[0].shape[1]
+    span = (fold_ref.shape[0] - 1) * 128
     lane = lax.broadcasted_iota(jnp.int32, (rows, SCALE_LANES), 1)
     tail = jnp.zeros((rows, SCALE_LANES), jnp.float32)
-    for n, part in enumerate(parts):
+    for n, take in enumerate(parts):
+        part = take()
         exponent = wire_scale(part)
         scaled = part * jnp.exp2(exponent)
         tiles = span // 128
@@ -145,16 +146,22 @@
     copies = [pltpu.make_async_copy(a, b, sems.at[n]) for n, (a, b) in enumerate(zip(sources, targets))]
     for copy in copies:
         copy.start()
-    copies[0].wait()
-    copies[1].wait()
-    driven = key_ref[...].astype(jnp.float32) * value_ref[...].astype(jnp.float32)
-    copies[2].wait()
+
+    def signal():
+        copies[0].wait()
+        copies[1].wait()
+        return (key_ref[...].astype(jnp.float32) * value_ref[...].astype(jnp.float32)).T
+
+    def taps():
+        copies[2].wait()
+        return taps_ref[...].T
+
+    store_folded(outs[0], fold_ref, [signal, taps])
 
     @pl.when(lax.axis_index("section") % 2 == 0)
     def _():
         pl.delay(LAG_NANOS)
 
-    store_folded(outs[0], fold_ref, [driven.T, taps_ref[...].T])
     for copy in copies[3:]:
         copy.wait()
 

time: 58 us -> 58 us (level)
  no operation moved by 1% of the time
where the time goes in v4:
time: 58 us; the launch traced here: 57.8 us
  blocking collectives  39 us (67%)
  starting transfers between devices  8.83 us (15%)
  Pallas kernels  4.82 us (8%)
  waiting for transfers between devices  3.32 us (6%)
  local copies, waits for them, and re-layouts  1.52 us (3%)
    all_to_all x2, blocking collectives, regrouped(): lax.all_to_all(blocks, 'seq', split_axis=0, concat_axis=0, tiled=True)  39 us
    ppermute x1, starting transfers between devices, passed_along(): lax.ppermute(value, axis, [(i, (i + by) % length) for i in range(length)])  8.83 us
    ppermute x1, waiting for transfers between devices, passed_along(): lax.ppermute(value, axis, [(i, (i + by) % length) for i in range(length)])  3.32 us
    pallas_call x1, Pallas kernels, on_device(): call(convolve_kernel, (rows, FOLD * span + SCALE_LANES), jnp.float32, 'co...  2.65 us
    pallas_call x1, Pallas kernels, on_device(): pl.pallas_call(pack_kernel, out_shape=[wire] + [jax.ShapeDtypeStruct(a.sh...  1.82 us
  transfers between devices with their start and end apart: 1, of which 1 were waited for; matrix products, arithmetic and copies ran while one was open for 0% of the time, Pallas kernels for 0%

profile of v4, /device:TPU:193, one launch (start us, length us, event | category | flops | bytes accessed | tf_op | source)
XLA Modules:
  0.0 57.8 jit_solution(1830896372507519586)
XLA Ops:
  0.0 1.8 %pack.1 = (f32[64,4224]{1,0:T(8,128)S(1)}, bf16[4,128,192]{2,1,0:T(8,128)(2,1)S(1)}, bf16[64,384]{1,0:T(8,128)(2,1)S(1)}, bf16[512,256]{1,0:T(8,128)(2,1)S(1)}, ...) custom-call(bf16[512,256]{1,0:T(8,128)(2,1)} %key_ref.1, bf16[512,256]{1,0:T(8,128)(2,1)} %value_ref.1, ...), custom_call_target="tpu_custom_call" | custom-call | tf_op jit(solution)/shard_map/pack/pallas_call | solution.py:261
  1.8 0.1 convert_element_type.12
  1.9 0.3 reshape.12
  2.2 22.4 %all_to_all.10 = f16[32,2,4224]{2,1,0:T(2,128)(2,1)S(1)} all-to-all(f16[32,2,4224]{2,1,0:T(2,128)(2,1)S(1)} %reshape.12), channel_id=1, replica_groups=mesh['section'=16,'seq'=32] {'seq'}, dimensions={0} | all-to-all | bytes 1081344 | tf_op jit(solution)/shard_map/all_to_all | solution.py:21
  24.5 0.3 reshape.13
  24.8 0.1 convert_element_type.13.in_ref
  24.9 2.6 %convolve.1 = f32[64,2176]{1,0:T(8,128)S(1)} custom-call(f32[64,4224]{1,0:T(8,128)S(1)} %convert_element_type.13.in_ref, bf16[4,128,192]{2,1,0:T(8,128)(2,1)S(1)} %get-tuple-element.12.rows_ref, bf16[64,384]{1,0:T(8,128)(2,1)S(1)} %get-tuple-element.13.back_ref, bf16[512,256]{1,0:T(8,128)(2,1)S(1)} %get-tuple-element.14.lanes_ref, ...), custom_call_target="tpu_custom_call" | custom-call | tf_op jit(solution)/shard_map/convolve/pallas_call | solution.py:276
  27.6 0.1 reshape.14
  27.7 0.0 copy-start
  27.7 0.0 copy-start.1
  27.7 0.0 copy-start.2
  27.7 0.0 copy-start.3
  27.8 16.6 %all_to_all.11 = f16[32,2,2176]{2,1,0:T(2,128)(2,1)S(1)} all-to-all(f16[32,2,2176]{2,1,0:T(2,128)(2,1)S(1)} %reshape.14), channel_id=1, replica_groups=mesh['section'=16,'seq'=32] {'seq'}, dimensions={0} | all-to-all | bytes 557056 | tf_op jit(solution)/shard_map/all_to_all | solution.py:21
  44.4 0.1 reshape.15
  44.5 0.0 copy-done
  44.6 0.0 copy-done.1
  44.6 0.0 copy-done.2
  44.6 0.0 copy-done.3
  44.6 0.4 mix.1
  45.0 8.8 %collective-permute-start = (bf16[512,256]{1,0:T(8,128)(2,1)S(1)}, bf16[512,256]{1,0:T(8,128)(2,1)S(1)}, u32[]{:S(2)}, u32[]{:S(2)}) collective-permute-start(bf16[512,256]{1,0:T(8,128)(2,1)S(1)} %mix.1), channel_id=1, source_target_pairs={{0,32},{32,64},{64,96},{96,128},{128,160},{160,192},{192,224},{224... | collective-permute-start | bytes 786440 | tf_op jit(solution)/shard_map/ppermute | solution.py:17
  53.8 3.3 %collective-permute-done = bf16[512,256]{1,0:T(8,128)(2,1)S(1)} collective-permute-done((bf16[512,256]{1,0:T(8,128)(2,1)S(1)}, bf16[512,256]{1,0:T(8,128)(2,1)S(1)}, u32[]{:S(2)}, u32[]{:S(2)}) %collective-permute-start) | collective-permute-done | bytes 262176 | tf_op jit(solution)/shard_map/ppermute | solution.py:17
  57.1 0.7 %copy.12 = bf16[512,256]{1,0:T(8,128)(2,1)} copy(bf16[512,256]{1,0:T(8,128)(2,1)S(1)} %collective-permute-done) | data formatting | bytes 524288
  (2 shorter events, 0.1 us)
Async XLA Ops:
  27.7 16.8 %copy-start = (bf16[512,256]{1,0:T(8,128)(2,1)S(1)}, bf16[512,256]{1,0:T(8,128)(2,1)}, u32[]{:S(2)}) copy-start(bf16[512,256]{1,0:T(8,128)(2,1)} %key_ref.1) | copy-start | bytes 786436
  27.7 16.8 %copy-start.1 = (bf16[512,256]{1,0:T(8,128)(2,1)S(1)}, bf16[512,256]{1,0:T(8,128)(2,1)}, u32[]{:S(2)}) copy-start(bf16[512,256]{1,0:T(8,128)(2,1)} %value_ref.1) | copy-start | bytes 786436
  27.7 16.8 %copy-start.2 = (bf16[512,256]{1,0:T(8,128)(2,1)S(1)}, bf16[512,256]{1,0:T(8,128)(2,1)}, u32[]{:S(2)}) copy-start(bf16[512,256]{1,0:T(8,128)(2,1)} %query_ref.1) | copy-start | bytes 786436
  27.7 16.8 %copy-start.3 = (f32[256]{0:T(256)S(1)}, f32[256]{0:T(256)}, u32[]{:S(2)}) copy-start(f32[256]{0:T(256)} %param.14) | copy-start | bytes 3076
  45.0 12.1 %collective-permute-start = (bf16[512,256]{1,0:T(8,128)(2,1)S(1)}, bf16[512,256]{1,0:T(8,128)(2,1)S(1)}, u32[]{:S(2)}, u32[]{:S(2)}) collective-permute-start(bf16[512,256]{1,0:T(8,128)(2,1)S(1)} %mix.1), channel_id=1, source_target_pairs={{0,32},{32,64},{64,96},{96,128},{128,160},{160,192},{192,224},{224... | collective-permute-start | bytes 786440 | tf_op jit(solution)/shard_map/ppermute | solution.py:17
